TPU v7x, 32 devices: a whole 2x2x4 slice. The times are simulated.
32 devices in a mesh: gx: 4 (over y, core), yz: 8 (over z, x).
Axes of the slice: x: 2, y: 2, z: 4, core: 2. Of those that a mesh axis runs over, the one named last changes fastest.
Arguments:
- composition: float32 [4096, 20, 128], P(('gx', 'yz')), may hold values from -6 to 6
- particle_mass: float32 [4096, 128], P(('gx', 'yz')), may hold values from 0.5 to 2
- mixing_rate: float32 [4096, 128], P(('gx', 'yz')), may hold values from 0.2 to 3
- cell_index: int32 [4096, 128], P(('gx', 'yz')), may hold values from 0 to 4095, as said below
- section_counts: int32 [4096], P(('gx', 'yz')), may hold values from 1 to 6, as said below
- block_shuffle: int32 [32, 128], P(('gx', 'yz')), may hold values from 0 to 127, as said below
- batch_inverse: float32 [32, 20, 20], P(('gx', 'yz')), may hold values from -1.25 to 1.25
- rate_exponents: float32 [84, 20], replicated, may hold values from -1.25 to 1.25
- stoichiometry: float32 [20, 84], replicated, may hold values from -0.625 to 0.625
Outputs:
- reacted: float32 [4096, 20, 128], P(('gx', 'yz'))
Inputs may be any that keep to these rules, and one draw needn't show every extreme that they name: `cell_index`: A particle of the device at index i of gx and j of yz (d = i * 8 + j) lies in slab i - 1, i or i + 1, slab s holding cells s * 128 * 8 to (s + 1) * 128 * 8 - 1; that device's first 128 particles lie one each in cells d * 128 to d * 128 + 127. `section_counts`: some block has exactly 6 sections. `block_shuffle`: each row is a permutation of 0 to 127.
All inputs are finite; a program needn't handle non-finite values.
Results may differ from a plain program's by a relative error of at most 0.0011.
Values sent between devices are 32-bit elements; how exact they have to be, the bound alone decides.
No kernel may reach another device: no remote copies, remote signals or barrier semaphores. Data moves between devices by JAX's collectives and lax.ppermute only.
A program may use at most 128 MiB of HBM per device.

v0:
```python
import functools

import jax
import jax.numpy as jnp
from jax import lax
from jax.experimental import pallas as pl
from jax.experimental.pallas import tpu as pltpu
from jax.sharding import PartitionSpec as P


STEP = 0.25
CELL_DEV = 128
SMAX = 6
LOW = 256
BF16 = jnp.bfloat16
F32 = jnp.float32


def round_up(value, multiple):
    return -(-value // multiple) * multiple


def split_in_two(values):
    upper = values.astype(BF16).astype(F32)
    return upper, values - upper


def moments_kernel(place_ref, comp_ref, mass_ref, cell_ref, out_ref, acc_ref, *, high, rows):
    step = pl.program_id(0)
    species, step_blocks, lanes = comp_ref.shape
    flat = comp_ref.reshape(species * step_blocks, lanes)

    @pl.when(step == 0)
    def _():
        acc_ref[...] = jnp.zeros_like(acc_ref)

    iota_low = lax.broadcasted_iota(jnp.int32, (LOW, lanes), 0).astype(F32).astype(BF16)
    local = cell_ref[...] - place_ref[0]
    hi = (local // LOW).astype(F32)
    lo = (local % LOW).astype(F32)
    zeros = jnp.zeros((rows - species - 1, lanes), F32)
    tables, spreads = [], []
    for b in range(step_blocks):
        m = mass_ref[b : b + 1, :]
        w = flat[pl.ds(b, species, stride=step_blocks), :] * m
        v = jnp.concatenate([w, m, zeros], axis=0)
        upper = v.astype(BF16).astype(F32)
        pieces = jnp.concatenate([upper, v - upper], axis=0).astype(BF16)
        low_row = jnp.broadcast_to(lo[b : b + 1, :], (LOW, lanes)).astype(BF16)
        tables.append(jnp.where(low_row == iota_low, BF16(1), BF16(0)))
        high_row = jnp.broadcast_to(hi[b : b + 1, :], (2 * rows, lanes)).astype(BF16)
        spreads.append(
            jnp.concatenate(
                [jnp.where(high_row == BF16(h), pieces, BF16(0)) for h in range(high)], axis=0
            )
        )
    table = jnp.concatenate(tables, axis=1)
    spread = jnp.concatenate(spreads, axis=1)
    acc_ref[...] += lax.dot_general(
        spread, table, (((1,), (1,)), ((), ())), preferred_element_type=F32
    )

    @pl.when(step == pl.num_programs(0) - 1)
    def _():
        per = high // 3
        width = per * LOW // lanes
        kept = species + 1
        out_flat = out_ref.reshape(3 * kept * width, lanes)
        for h in range(high):
            top = h * 2 * rows
            slab = h // per
            slot = 0 if slab == 1 else place_ref[1 + slab // 2]
            for c in range(LOW // lanes):
                cols = slice(c * lanes, (c + 1) * lanes)
                total = acc_ref[top : top + rows, cols] + acc_ref[top + rows : top + 2 * rows, cols]
                start = slot * kept * width + (h % per) * (LOW // lanes) + c
                out_flat[pl.ds(start, kept, stride=width), :] = total[:kept]


def moments(place, comp, mass, cell, slab_cells, rows):
    species, blocks, lanes = comp.shape
    high = 3 * slab_cells // LOW
    step_blocks = min(64, blocks)
    sums = (species + 1) * slab_cells // lanes
    return pl.pallas_call(
        functools.partial(moments_kernel, high=high, rows=rows),
        out_shape=jax.ShapeDtypeStruct((3, sums, lanes), F32),
        grid_spec=pltpu.PrefetchScalarGridSpec(
            num_scalar_prefetch=1,
            grid=(blocks // step_blocks,),
            in_specs=[
                pl.BlockSpec((species, step_blocks, lanes), lambda s, p: (0, s, 0)),
                pl.BlockSpec((step_blocks, lanes), lambda s, p: (s, 0)),
                pl.BlockSpec((step_blocks, lanes), lambda s, p: (s, 0)),
            ],
            out_specs=pl.BlockSpec((3, sums, lanes), lambda s, p: (0, 0, 0)),
            scratch_shapes=[pltpu.VMEM((2 * rows * high, LOW), F32)],
        ),
        compiler_params=pltpu.CompilerParams(vmem_limit_bytes=48 << 20),
        cost_estimate=pl.CostEstimate(
            flops=2 * blocks * lanes * high * LOW * 2 * rows, bytes_accessed=4 * comp.size, transcendentals=0
        ),
        name="moments",
    )(place, comp, mass, cell)


def react_kernel(
    length_ref, sched_ref, batch_ref, place_ref,
    own_ref, near_ref, far_ref, comp_ref, rate_ref, cell_ref, rates_ref, net_ref,
    out_ref, table_ref, state_ref, *, group, slots, chunk,
):
    species, blocks, lanes = comp_ref.shape
    width = own_ref.shape[0] // (species + 1)
    rows = state_ref.shape[1]
    flat = comp_ref.reshape(species * blocks, lanes)
    out_flat = out_ref.reshape(species * blocks, lanes)
    parts = LOW // lanes
    per = width // parts
    high = 3 * per
    first = place_ref[0]
    left_near = place_ref[1] == 1
    half = rows - species

    for h in range(high):
        slab = h // per

        def cells(ref):
            start = (h % per) * parts
            return jnp.concatenate(
                [ref[pl.ds(start + c, species + 1, stride=width), :] for c in range(parts)], axis=1
            )

        if slab == 1:
            t = cells(own_ref)
        elif slab == 0:
            t = jnp.where(left_near, cells(near_ref), cells(far_ref))
        else:
            t = jnp.where(left_near, cells(far_ref), cells(near_ref))
        m = t[species : species + 1, :]
        mean = jnp.where(m > 0, t[:species] / m, 0.0)
        for side, piece in enumerate(split_in_two(mean)):
            top = side * species * high
            table_ref[top + h * 16 : top + h * 16 + 16] = piece[:16]
            rest_top = top + 16 * high + half * h
            table_ref[rest_top : rest_top + half] = piece[16:]

    iota_low = lax.broadcasted_iota(jnp.int32, (LOW, lanes), 0).astype(F32).astype(BF16)

    second = lax.broadcasted_iota(jnp.int32, (2 * half, lanes), 0) // half

    def mix_group(g, carry):
        base = g * group
        hots, his = [], []
        for j in range(group):
            local = cell_ref[pl.ds(base + j, 1), :] - first
            low_row = jnp.broadcast_to((local % LOW).astype(F32), (LOW, lanes)).astype(BF16)
            his.append(local // LOW)
            hots.append(jnp.where(low_row == iota_low, BF16(1), BF16(0)))
        hot = jnp.concatenate(hots, axis=1)
        picked = jnp.dot(table_ref[...].astype(BF16), hot, preferred_element_type=F32)
        picked = picked[: species * high] + picked[species * high :]
        for j in range(group):
            part = slice(j * lanes, (j + 1) * lanes)
            high_row = jnp.broadcast_to(his[j], (16, lanes))
            high_half = jnp.broadcast_to(his[j], (2 * half, lanes)) - second
            looked = jnp.where(high_row == 0, picked[0:16, part], 0.0)
            for h in range(1, high):
                looked = jnp.where(high_row == h, picked[h * 16 : h * 16 + 16, part], looked)
            rest = jnp.zeros((2 * half, lanes), F32)
            for h in range(0, high, 2):
                top = 16 * high + half * h
                rest = jnp.where(high_half == h, picked[top : top + 2 * half, part], rest)
            rest = rest + pltpu.roll(rest, half, 0)
            looked = jnp.concatenate([looked, rest], axis=0)
            decay = jnp.exp(-rate_ref[pl.ds(base + j, 1), :])
            c = flat[pl.ds(base + j, species, stride=blocks), :]
            c = jnp.concatenate([c, c[16:]], axis=0)
            state_ref[base + j] = looked + (c - looked) * decay
        return carry

    lax.fori_loop(0, blocks // group, mix_group, 0)
    state_ref[blocks] = jnp.zeros((rows, lanes), F32)
    length = length_ref[0]

    def section(s, carry):
        ids = [sched_ref[j * length + s] for j in range(slots)]
        held = []
        for c in range(0, slots, chunk):
            x = jnp.concatenate([state_ref[ids[c + j]] for j in range(chunk)], axis=1)
            upper, lower = split_in_two(x)
            k1 = jnp.concatenate([upper, lower, upper[:16]], axis=0).astype(BF16)
            t = jnp.tanh(jnp.dot(rates_ref[...], k1, preferred_element_type=F32))
            held.append((x, jnp.concatenate(split_in_two(t), axis=0).astype(BF16)))
        for c in range(0, slots, chunk):
            x, k2 = held[c // chunk]
            for p in range(0, chunk, 2):
                pair = (ids[c + p], ids[c + p + 1])
                net = jnp.concatenate([net_ref[batch_ref[i]] for i in pair], axis=0)
                f = jnp.dot(net, k2[:, p * lanes : (p + 2) * lanes], preferred_element_type=F32)
                for i in range(2):
                    cols = slice(i * lanes, (i + 1) * lanes)
                    top = 2 * i * rows
                    change = f[top : top + rows, cols] + f[top + rows : top + 2 * rows, cols]
                    state_ref[pair[i]] = x[:, (p + i) * lanes : (p + i + 1) * lanes] + STEP * change
        return carry

    lax.fori_loop(0, length, section, 0)

    def put_out(g, carry):
        for j in range(group):
            out_flat[pl.ds(g * group + j, species, stride=blocks), :] = state_ref[g * group + j, :species, :]
        return carry

    lax.fori_loop(0, blocks // group, put_out, 0)


def react(length, sched, batch, place, own, near, far, comp, rate, cell, rates, net, slots):
    species, blocks, lanes = comp.shape
    rows = round_up(species + 1, 8)
    high = 3 * (own.shape[0] * lanes // (species + 1)) // LOW
    vmem = pl.BlockSpec(memory_space=pltpu.VMEM)
    return pl.pallas_call(
        functools.partial(react_kernel, group=min(128, blocks), slots=slots, chunk=8),
        out_shape=jax.ShapeDtypeStruct(comp.shape, F32),
        grid_spec=pltpu.PrefetchScalarGridSpec(
            num_scalar_prefetch=4,
            grid=(),
            in_specs=[vmem] * 8,
            out_specs=vmem,
            scratch_shapes=[
                pltpu.VMEM((2 * species * high, LOW), F32),
                pltpu.VMEM((blocks + 1, rows, lanes), F32),
            ],
        ),
        compiler_params=pltpu.CompilerParams(vmem_limit_bytes=28 << 20),
        cost_estimate=pl.CostEstimate(
            flops=2 * blocks * lanes * high * LOW * 2 * rows, bytes_accessed=8 * comp.size, transcendentals=0
        ),
        name="react",
    )(length, sched, batch, place, own, near, far, comp, rate, cell, rates, net)


def split_two(values):
    upper = lax.reduce_precision(values, 8, 7)
    return upper, lax.reduce_precision(values - upper, 8, 7)


def pack_rates(rates, rows, steps):
    reactions, species = rates.shape
    spare = 2 * species - rows
    upper, lower = split_two(jnp.pad(rates, ((0, steps - reactions), (0, 0))))
    zeros = jnp.zeros((steps, rows - species), F32)
    return jnp.concatenate([upper, lower[:, spare:], upper, zeros, lower[:, :spare]], axis=1).astype(BF16)


def pack_net(inverse, stoichiometry, rows, steps):
    species = inverse.shape[1]
    reactions = stoichiometry.shape[1]
    inverse = jnp.concatenate([inverse, inverse[:, 2 * species - rows :]], axis=1)
    stoichiometry = jnp.pad(stoichiometry, ((0, 0), (0, steps - reactions)))
    net = jnp.einsum("qij,jr->qir", inverse, stoichiometry, precision=lax.Precision.HIGHEST)
    upper, lower = split_two(net)
    return jnp.concatenate(
        [jnp.concatenate([upper, upper], axis=2), jnp.concatenate([lower, jnp.zeros_like(lower)], axis=2)],
        axis=1,
    ).astype(BF16)


def section_schedule(counts, slots):
    blocks = counts.shape[0]
    ids = jnp.arange(blocks, dtype=jnp.int32)
    ends = jnp.sum(jnp.where(ids[None, :] <= ids[:, None], counts[None, :], 0), axis=1)
    total = jnp.sum(counts)
    length = jnp.maximum(jnp.max(counts), (total + slots - 1) // slots)
    places = jnp.arange(round_up(SMAX * blocks + slots, 128), dtype=jnp.int32)
    sched = jnp.sum((ends[:, None] <= places[None, :]).astype(jnp.int32), axis=0)
    return length.reshape(1).astype(jnp.int32), sched


def flat_inverses(inverses, lanes):
    count = inverses.shape[0]
    size = inverses.shape[1] * inverses.shape[2]
    flat = jnp.pad(inverses.reshape(count, size), ((0, 0), (0, round_up(size, lanes) - size)))
    return flat.reshape(-1, lanes)


def from_partner(values, mask):
    count = lax.axis_size("yz")
    return lax.ppermute(values, "yz", [(i, i ^ mask) for i in range(count)])


def swap_pairs(near, far):
    count = lax.axis_size("gx")
    first = [(i, i ^ 1) for i in range(count) if i ^ 1 < count]
    second = [(i, i - 1 if i % 2 == 0 else i + 1) for i in range(count)]
    second = [(i, j) for i, j in second if 0 <= j < count]
    near = lax.ppermute(near, "gx", first)
    far = lax.ppermute(far, "gx", second)
    return near, far


def local(
    composition, particle_mass, mixing_rate, cell_index, section_counts, block_shuffle,
    batch_inverse, rate_exponents, stoichiometry,
):
    blocks, species, lanes = composition.shape
    reactions = rate_exponents.shape[0]
    slabs, columns = lax.axis_size("gx"), lax.axis_size("yz")
    devices = slabs * columns
    slab_cells = CELL_DEV * columns
    rows = round_up(species + 1, 8)
    steps = round_up(reactions, 8)
    slab, column = lax.axis_index("gx"), lax.axis_index("yz")
    odd = slab % 2
    place = jnp.stack([(slab - 1) * slab_cells, 2 - odd, 1 + odd]).astype(jnp.int32)

    inverses = [batch_inverse]
    for distance in range(1, slabs):
        inverses.append(lax.ppermute(batch_inverse, "gx", [(i, i ^ distance) for i in range(slabs)]))
    bits = [1 << k for k in range((columns - 1).bit_length())]
    comp = jnp.transpose(composition, (1, 0, 2))
    held = [pltpu.with_memory_space_constraint(v, pltpu.HBM) for v in (comp, particle_mass, cell_index)]
    partial = moments(place, *held, slab_cells, rows)
    near, far = partial[1], partial[2]
    got_near, got_far = swap_pairs(near, far)
    inverses = flat_inverses(jnp.concatenate(inverses, axis=0), lanes)
    own = partial[0] + got_near + got_far
    sums = own.shape[0]
    for at in range(0, len(bits), 2):
        message = jnp.concatenate([own, inverses], axis=0)
        masks = [sum(m) for m in ([bits[at]], bits[at + 1 : at + 2], bits[at : at + 2])]
        got = [from_partner(message, m) for m in (masks if at + 1 < len(bits) else masks[:1])]
        own = sum((g[:sums] for g in got), own)
        inverses = jnp.concatenate([inverses] + [g[sums:] for g in got], axis=0)
    near, far = swap_pairs(own, own)

    block_ids = jnp.arange(blocks, dtype=jnp.int32)
    slots = min(32, blocks)
    length, sched = section_schedule(section_counts, slots)
    slot = jnp.sum(
        jnp.where(block_shuffle[0][:, None] == block_ids[None, :], block_ids[:, None], 0), axis=0
    )
    batch = (slot // (blocks // devices)) ^ (slab * columns + column)
    batch = batch % columns * slabs + batch // columns
    batch = jnp.pad(batch, (0, 128))
    size = species * species
    matrices = inverses.reshape(devices, -1)[:, :size].reshape(devices, species, species)
    rates = pack_rates(rate_exponents, rows, steps)
    net = pack_net(matrices, stoichiometry, rows, steps)
    out = react(
        length, sched, batch, place, own, near, far, comp, mixing_rate, cell_index, rates, net, slots
    )
    return jnp.transpose(out, (1, 0, 2))


def solution(mesh):
    both = ("gx", "yz")
    in_specs = (
        P(both, None, None),
        P(both, None),
        P(both, None),
        P(both, None),
        P(both),
        P(both, None),
        P(both, None, None),
        P(),
        P(),
    )
    return jax.shard_map(local, mesh=mesh, in_specs=in_specs, out_specs=P(both, None, None), check_vma=False)
```

profile of v0, /device:TPU:0, one launch (start us, length us, event | category | flops | bytes accessed | tf_op | source)
XLA Modules:
  0.0 52.9 jit_solution(2364877326148090720)
XLA Ops:
  0.0 3.0 %collective-permute-start.3 = (f32[1,20,20]{2,0,1:T(1,128)}, f32[1,20,20]{2,0,1:T(1,128)S(1)}, u32[]{:S(2)}, u32[]{:S(2)}) collective-permute-start(f32[1,20,20]{2,0,1:T(1,128)} %param.15), channel_id=1, source_target_pairs={{0,16},{8,24},{16,0},{24,8},{1,17},{9,25},{17,1},{25,9},{2,18},{10... | collective-permute-start | bytes 4808 | tf_op jit(solution)/shard_map/ppermute | solution.py:319
  3.0 0.1 collective-permute-start.4
  3.1 0.1 pad_add_fusion.place_ref
  3.2 7.1 %moments.1 = f32[3,168,128]{2,1,0:T(8,128)S(1)} custom-call(s32[3]{0:T(128)S(1)} %pad_add_fusion.place_ref, f32[20,128,128]{2,1,0:T(8,128)} %bitcast.27, f32[128,128]{1,0:T(8,128)} %mass_ref.1, s32[128,128]{1,0:T(8,128)} %cell_ref.3), custom_call_target="tpu_custom_call" | custom-call | flops 4831838208 | bytes 1310720 | tf_op jit(solution)/shard_map/moments/pallas_call | solution.py:85
  10.3 0.5 collective-permute-start
  10.7 0.7 %collective-permute-start.1 = (f32[168,128]{1,0:T(8,128)S(1)}, f32[168,128]{1,0:T(8,128)S(1)}, u32[]{:S(2)}, u32[]{:S(2)}) collective-permute-start(f32[168,128]{1,0:T(8,128)S(1)} %get-tuple-element.12), channel_id=1, source_target_pairs={{8,16},{16,8},{9,17},{17,9},{10,18},{18,10},{11,19},{19,11},{12,20... | collective-permute-start | bytes 258056 | tf_op jit(solution)/shard_map/ppermute | solution.py:298
  11.4 0.1 select_reduce_fusion
  11.5 0.1 select_reduce_fusion.1
  11.7 0.6 %fusion.14 = (s32[]{:T(128)}, s32[]{:T(128)}) fusion(s32[128]{0:T(128)S(1)} %copy-done.7), kind=kLoop, calls=%fused_computation.55 | loop fusion | flops 254 | bytes 520 | tf_op jit(solution)/shard_map/reduce_sum | solution.py:273
  13.0 0.1 copy.20
  13.1 0.1 pad_maximum_fusion.2
  13.2 0.1 reshape.19
  13.4 2.7 %collective-permute-start.7 = (f32[184,128]{1,0:T(8,128)S(1)}, f32[184,128]{1,0:T(8,128)S(1)}, u32[]{:S(2)}, u32[]{:S(2)}) collective-permute-start(f32[184,128]{1,0:T(8,128)S(1)} %pad_maximum_fusion.1), channel_id=1, source_target_pairs={{0,3},{1,2},{2,1},{3,0},{4,7},{5,6},{6,5},{7,4},{8,11},{9,10},{10,... | collective-permute-start | bytes 282632 | tf_op jit(solution)/shard_map/ppermute | solution.py:289
  16.1 0.4 collective-permute-start.6
  16.5 0.4 collective-permute-start.5
  17.0 2.0 %collective-permute-done.7 = f32[184,128]{1,0:T(8,128)S(1)} collective-permute-done((f32[184,128]{1,0:T(8,128)S(1)}, f32[184,128]{1,0:T(8,128)S(1)}, u32[]{:S(2)}, u32[]{:S(2)}) %collective-permute-start.7) | collective-permute-done | bytes 94240 | tf_op jit(solution)/shard_map/ppermute | solution.py:289
  18.9 1.7 %collective-permute-done.6 = f32[184,128]{1,0:T(8,128)S(1)} collective-permute-done((f32[184,128]{1,0:T(8,128)S(1)}, f32[184,128]{1,0:T(8,128)S(1)}, u32[]{:S(2)}, u32[]{:S(2)}) %collective-permute-start.6) | collective-permute-done | bytes 94240 | tf_op jit(solution)/shard_map/ppermute | solution.py:289
  20.7 1.5 %collective-permute-done.5 = f32[184,128]{1,0:T(8,128)S(1)} collective-permute-done((f32[184,128]{1,0:T(8,128)S(1)}, f32[184,128]{1,0:T(8,128)S(1)}, u32[]{:S(2)}, u32[]{:S(2)}) %collective-permute-start.5) | collective-permute-done | bytes 94240 | tf_op jit(solution)/shard_map/ppermute | solution.py:289
  22.2 2.7 %collective-permute-start.8 = (f32[232,128]{1,0:T(8,128)S(1)}, f32[232,128]{1,0:T(8,128)S(1)}, u32[]{:S(2)}, u32[]{:S(2)}) collective-permute-start(f32[232,128]{1,0:T(8,128)S(1)} %get-tuple-element.14), channel_id=1, source_target_pairs={{0,4},{1,5},{2,6},{3,7},{4,0},{5,1},{6,2},{7,3},{8,12},{9,13},{10,... | collective-permute-start | bytes 356360 | tf_op jit(solution)/shard_map/ppermute | solution.py:289
  24.9 0.1 slice.72
  25.5 0.1 concatenate.36.rates_ref
  25.6 0.1 convert_reduce_fusion.sched_ref
  25.8 6.0 %collective-permute-done.8 = f32[232,128]{1,0:T(8,128)S(1)} collective-permute-done((f32[232,128]{1,0:T(8,128)S(1)}, f32[232,128]{1,0:T(8,128)S(1)}, u32[]{:S(2)}, u32[]{:S(2)}) %collective-permute-start.8) | collective-permute-done | bytes 118816 | tf_op jit(solution)/shard_map/ppermute | solution.py:289
  31.8 0.7 %collective-permute-start.10 = (f32[168,128]{1,0:T(8,128)S(1)}, f32[168,128]{1,0:T(8,128)S(1)}, u32[]{:S(2)}, u32[]{:S(2)}) collective-permute-start(f32[168,128]{1,0:T(8,128)S(1)} %slice_add_fusion.own_ref), channel_id=1, source_target_pairs={{8,16},{16,8},{9,17},{17,9},{10,18},{18,10},{11,19},{19,11},{12,20... | collective-permute-start | bytes 258056 | tf_op jit(solution)/shard_map/ppermute | solution.py:298
  32.5 3.2 %collective-permute-start.9 = (f32[168,128]{1,0:T(8,128)S(1)}, f32[168,128]{1,0:T(8,128)S(1)}, u32[]{:S(2)}, u32[]{:S(2)}) collective-permute-start(f32[168,128]{1,0:T(8,128)S(1)} %slice_add_fusion.own_ref), channel_id=1, source_target_pairs={{0,8},{8,0},{16,24},{24,16},{1,9},{9,1},{17,25},{25,17},{2,10},{10... | collective-permute-start | bytes 258056 | tf_op jit(solution)/shard_map/ppermute | solution.py:297
  35.7 0.1 copy.26
  35.9 0.0 copy-start.1
  36.0 0.0 copy-start.2
  36.0 0.2 copy.24
  36.2 0.8 %reduce-precision_convert_fusion = (bf16[32,24,88]{2,1,0:T(8,128)(2,1)S(1)}, bf16[32,24,88]{2,1,0:T(8,128)(2,1)S(1)}) fusion(f32[32,24,20]{1,2,0:T(8,128)S(1)} %copy.24, f32[20,84]{1,0:T(8,128)S(1)} %copy-done.4), kind=kOutput, calls=%fused_computation.4 | convolution fusion | flops 16558080 | bytes 338496 | tf_op jit(solution)/shard_map/qij,jr->qir/dot_general | solution.py:261
  37.0 0.2 fusion.1.net_ref
  37.3 15.6 %react.1 = f32[20,128,128]{2,1,0:T(8,128)} custom-call(s32[1]{0:T(128)} %bitcast.length_ref, s32[896]{0:T(1024)S(1)} %convert_reduce_fusion.sched_ref, s32[256]{0:T(256)S(1)} %pad.18.batch_ref, s32[3]{0:T(128)S(1)} %pad_add_fusion.place_ref, f32[168,128]{1,0:T(8,128)S(1)} %slice_add_fusion.own_ref, f32[168,128]{1,0:T(8,128)S(1)} %collective-permute-done.9.near_ref, ...), custom_call_target="tpu_custom_call" | custom-call | flops 4831838208 | bytes 2621440 | tf_op jit(solution)/shard_map/react/pallas_call | solution.py:222
  (43 shorter events, 0.3 us)
Async XLA Ops:
  0.0 13.1 %collective-permute-start.3 = (f32[1,20,20]{2,0,1:T(1,128)}, f32[1,20,20]{2,0,1:T(1,128)S(1)}, u32[]{:S(2)}, u32[]{:S(2)}) collective-permute-start(f32[1,20,20]{2,0,1:T(1,128)} %param.15), channel_id=1, source_target_pairs={{0,16},{8,24},{16,0},{24,8},{1,17},{9,25},{17,1},{25,9},{2,18},{10... | collective-permute-start | bytes 4808 | tf_op jit(solution)/shard_map/ppermute | solution.py:319
  3.0 10.1 %collective-permute-start.2 = (f32[1,20,20]{2,0,1:T(1,128)}, f32[1,20,20]{2,0,1:T(1,128)S(1)}, u32[]{:S(2)}, u32[]{:S(2)}) collective-permute-start(f32[1,20,20]{2,0,1:T(1,128)} %param.15), channel_id=1, source_target_pairs={{0,8},{8,0},{16,24},{24,16},{1,9},{9,1},{17,25},{25,17},{2,10},{10... | collective-permute-start | bytes 4808 | tf_op jit(solution)/shard_map/ppermute | solution.py:319
  3.0 10.1 %collective-permute-start.4 = (f32[1,20,20]{2,0,1:T(1,128)}, f32[1,20,20]{2,0,1:T(1,128)S(1)}, u32[]{:S(2)}, u32[]{:S(2)}) collective-permute-start(f32[1,20,20]{2,0,1:T(1,128)} %param.15), channel_id=1, source_target_pairs={{0,24},{8,16},{16,8},{24,0},{1,25},{9,17},{17,9},{25,1},{2,26},{10... | collective-permute-start | bytes 4808 | tf_op jit(solution)/shard_map/ppermute | solution.py:319
  3.2 8.2 %copy-start.6 = (s32[1,128]{1,0:T(1,128)S(1)}, s32[1,128]{1,0:T(1,128)}, u32[]{:S(2)}) copy-start(s32[1,128]{1,0:T(1,128)} %param.14) | copy-start | bytes 1540
  3.2 8.3 %copy-start.7 = (s32[128]{0:T(128)S(1)}, s32[128]{0:T(128)}, u32[]{:S(2)}) copy-start(s32[128]{0:T(128)} %param.13) | copy-start | bytes 1540
  3.2 9.8 %copy-start.3 = (f32[84,20]{0,1:T(8,128)S(1)}, f32[84,20]{0,1:T(8,128)}, u32[]{:S(2)}) copy-start(f32[84,20]{0,1:T(8,128)} %param.16) | copy-start | bytes 20164
  3.2 9.9 %copy-start.5 = (f32[1,20,20]{2,0,1:T(1,128)S(1)}, f32[1,20,20]{2,0,1:T(1,128)}, u32[]{:S(2)}) copy-start(f32[1,20,20]{2,0,1:T(1,128)} %param.15) | copy-start | bytes 4804
  10.3 3.0 %collective-permute-start = (f32[168,128]{1,0:T(8,128)S(1)}, f32[168,128]{1,0:T(8,128)S(1)}, u32[]{:S(2)}, u32[]{:S(2)}) collective-permute-start(f32[168,128]{1,0:T(8,128)S(1)} %get-tuple-element.11), channel_id=1, source_target_pairs={{0,8},{8,0},{16,24},{24,16},{1,9},{9,1},{17,25},{25,17},{2,10},{10... | collective-permute-start | bytes 258056 | tf_op jit(solution)/shard_map/ppermute | solution.py:297
  10.7 2.6 %collective-permute-start.1 = (f32[168,128]{1,0:T(8,128)S(1)}, f32[168,128]{1,0:T(8,128)S(1)}, u32[]{:S(2)}, u32[]{:S(2)}) collective-permute-start(f32[168,128]{1,0:T(8,128)S(1)} %get-tuple-element.12), channel_id=1, source_target_pairs={{8,16},{16,8},{9,17},{17,9},{10,18},{18,10},{11,19},{19,11},{12,20... | collective-permute-start | bytes 258056 | tf_op jit(solution)/shard_map/ppermute | solution.py:298
  13.4 5.5 %collective-permute-start.7 = (f32[184,128]{1,0:T(8,128)S(1)}, f32[184,128]{1,0:T(8,128)S(1)}, u32[]{:S(2)}, u32[]{:S(2)}) collective-permute-start(f32[184,128]{1,0:T(8,128)S(1)} %pad_maximum_fusion.1), channel_id=1, source_target_pairs={{0,3},{1,2},{2,1},{3,0},{4,7},{5,6},{6,5},{7,4},{8,11},{9,10},{10,... | collective-permute-start | bytes 282632 | tf_op jit(solution)/shard_map/ppermute | solution.py:289
  16.1 4.6 %collective-permute-start.6 = (f32[184,128]{1,0:T(8,128)S(1)}, f32[184,128]{1,0:T(8,128)S(1)}, u32[]{:S(2)}, u32[]{:S(2)}) collective-permute-start(f32[184,128]{1,0:T(8,128)S(1)} %pad_maximum_fusion.1), channel_id=1, source_target_pairs={{0,2},{1,3},{2,0},{3,1},{4,6},{5,7},{6,4},{7,5},{8,10},{9,11},{10,... | collective-permute-start | bytes 282632 | tf_op jit(solution)/shard_map/ppermute | solution.py:289
  16.5 5.6 %collective-permute-start.5 = (f32[184,128]{1,0:T(8,128)S(1)}, f32[184,128]{1,0:T(8,128)S(1)}, u32[]{:S(2)}, u32[]{:S(2)}) collective-permute-start(f32[184,128]{1,0:T(8,128)S(1)} %pad_maximum_fusion.1), channel_id=1, source_target_pairs={{0,1},{1,0},{2,3},{3,2},{4,5},{5,4},{6,7},{7,6},{8,9},{9,8},{10,11... | collective-permute-start | bytes 282632 | tf_op jit(solution)/shard_map/ppermute | solution.py:289
  22.2 9.6 %collective-permute-start.8 = (f32[232,128]{1,0:T(8,128)S(1)}, f32[232,128]{1,0:T(8,128)S(1)}, u32[]{:S(2)}, u32[]{:S(2)}) collective-permute-start(f32[232,128]{1,0:T(8,128)S(1)} %get-tuple-element.14), channel_id=1, source_target_pairs={{0,4},{1,5},{2,6},{3,7},{4,0},{5,1},{6,2},{7,3},{8,12},{9,13},{10,... | collective-permute-start | bytes 356360 | tf_op jit(solution)/shard_map/ppermute | solution.py:289
  25.6 10.5 %copy-start.4 = (f32[20,84]{1,0:T(8,128)S(1)}, f32[20,84]{1,0:T(8,128)}, u32[]{:S(2)}) copy-start(f32[20,84]{1,0:T(8,128)} %param.17) | copy-start | bytes 20164
  31.8 5.4 %collective-permute-start.10 = (f32[168,128]{1,0:T(8,128)S(1)}, f32[168,128]{1,0:T(8,128)S(1)}, u32[]{:S(2)}, u32[]{:S(2)}) collective-permute-start(f32[168,128]{1,0:T(8,128)S(1)} %slice_add_fusion.own_ref), channel_id=1, source_target_pairs={{8,16},{16,8},{9,17},{17,9},{10,18},{18,10},{11,19},{19,11},{12,20... | collective-permute-start | bytes 258056 | tf_op jit(solution)/shard_map/ppermute | solution.py:298
  32.5 4.7 %collective-permute-start.9 = (f32[168,128]{1,0:T(8,128)S(1)}, f32[168,128]{1,0:T(8,128)S(1)}, u32[]{:S(2)}, u32[]{:S(2)}) collective-permute-start(f32[168,128]{1,0:T(8,128)S(1)} %slice_add_fusion.own_ref), channel_id=1, source_target_pairs={{0,8},{8,0},{16,24},{24,16},{1,9},{9,1},{17,25},{25,17},{2,10},{10... | collective-permute-start | bytes 258056 | tf_op jit(solution)/shard_map/ppermute | solution.py:297
  35.9 1.3 %copy-start = (f32[128,20,128]{2,0,1:T(8,128)S(1)}, f32[128,20,128]{2,0,1:T(8,128)}, u32[]{:S(2)}) copy-start(f32[128,20,128]{2,0,1:T(8,128)} %param.9) | copy-start | bytes 3932164
  35.9 1.3 %copy-start.1 = (s32[128,128]{1,0:T(8,128)S(1)}, s32[128,128]{1,0:T(8,128)}, u32[]{:S(2)}) copy-start(s32[128,128]{1,0:T(8,128)} %cell_ref.3) | copy-start | bytes 196612
  36.0 1.3 %copy-start.2 = (f32[128,128]{1,0:T(8,128)S(1)}, f32[128,128]{1,0:T(8,128)}, u32[]{:S(2)}) copy-start(f32[128,128]{1,0:T(8,128)} %rate_ref.1) | copy-start | bytes 196612
where the time goes:
time: 53.1 us; the launch traced here: 52.9 us
  Pallas kernels  22.6 us (43%)
  starting transfers between devices  14.3 us (27%)
  waiting for transfers between devices  11.2 us (21%)
  between operations  1.6 us (3%)
  other arithmetic  1.43 us (3%)
  local copies, waits for them, and re-layouts  0.87 us (2%)
  matrix products  0.8 us (2%)
    pallas_call x1, Pallas kernels, react(): pl.pallas_call(functools.partial(react_kernel, group=min(128, blocks), sl...  15.6 us
    ppermute x4, waiting for transfers between devices, from_partner(): return lax.ppermute(values, 'yz', [(i, i ^ mask) for i in range(count)])  11.2 us
    pallas_call x1, Pallas kernels, moments(): pl.pallas_call(functools.partial(moments_kernel, high=high, rows=rows), o...  7.05 us
    ppermute x4, starting transfers between devices, from_partner(): return lax.ppermute(values, 'yz', [(i, i ^ mask) for i in range(count)])  6.21 us
    ppermute x2, starting transfers between devices, swap_pairs(): near = lax.ppermute(near, 'gx', first)  3.67 us
    ppermute x3, starting transfers between devices, local(): lax.ppermute(batch_inverse, 'gx', [(i, i ^ distance) for i in range(slabs)])  3.11 us
    ppermute x2, starting transfers between devices, swap_pairs(): far = lax.ppermute(far, 'gx', second)  1.32 us
  transfers between devices with their start and end apart: 11, of which 4 were waited for; matrix products, arithmetic and copies ran while one was open for 6% of the time, Pallas kernels for 13%

commit v1 on v0

--- a/solution.py
+++ b/solution.py
@@ -107,13 +107,12 @@
 def react_kernel(
     length_ref, sched_ref, batch_ref, place_ref,
     own_ref, near_ref, far_ref, comp_ref, rate_ref, cell_ref, rates_ref, net_ref,
-    out_ref, table_ref, state_ref, *, group, slots, chunk,
+    out_ref, table_ref, state_ref, sem_ref, *, group, slots, chunk,
 ):
     species, blocks, lanes = comp_ref.shape
     width = own_ref.shape[0] // (species + 1)
     rows = state_ref.shape[1]
     flat = comp_ref.reshape(species * blocks, lanes)
-    out_flat = out_ref.reshape(species * blocks, lanes)
     parts = LOW // lanes
     per = width // parts
     high = 3 * per
@@ -206,12 +205,14 @@
 
     lax.fori_loop(0, length, section, 0)
 
-    def put_out(g, carry):
-        for j in range(group):
-            out_flat[pl.ds(g * group + j, species, stride=blocks), :] = state_ref[g * group + j, :species, :]
-        return carry
-
-    lax.fori_loop(0, blocks // group, put_out, 0)
+    copies = [
+        pltpu.make_async_copy(state_ref.at[pl.ds(0, blocks), n, :], out_ref.at[n], sem_ref.at[n])
+        for n in range(species)
+    ]
+    for copy in copies:
+        copy.start()
+    for copy in copies:
+        copy.wait()
 
 
 def react(length, sched, batch, place, own, near, far, comp, rate, cell, rates, net, slots):
@@ -226,10 +227,11 @@
             num_scalar_prefetch=4,
             grid=(),
             in_specs=[vmem] * 8,
-            out_specs=vmem,
+            out_specs=pl.BlockSpec(memory_space=pltpu.HBM),
             scratch_shapes=[
                 pltpu.VMEM((2 * species * high, LOW), F32),
                 pltpu.VMEM((blocks + 1, rows, lanes), F32),
+                pltpu.SemaphoreType.DMA((species,)),
             ],
         ),
         compiler_params=pltpu.CompilerParams(vmem_limit_bytes=28 << 20),

time: 53.1 us -> 52.1 us (0.981)
  Pallas kernels: 22.6 us -> 21.6 us
    pallas_call x1, Pallas kernels: 15.6 us -> 14.6 us  [react(): pl.pallas_call(functools.partial(react_kernel, group=min(128, blocks), sl...]
  transfers between devices with their start and end apart: 11 -> 11, of which waited for: 4 -> 4; matrix products, arithmetic and copies ran while one was open for 6% -> 6% of each run, Pallas kernels for 13% -> 14%
where the time goes in v1:
time: 52.1 us; the launch traced here: 51.9 us
  Pallas kernels  21.6 us (41%)
  starting transfers between devices  14.3 us (27%)
  waiting for transfers between devices  11.2 us (21%)
  between operations  1.6 us (3%)
  other arithmetic  1.43 us (3%)
  local copies, waits for them, and re-layouts  0.87 us (2%)
  matrix products  0.8 us (2%)
    pallas_call x1, Pallas kernels, react(): pl.pallas_call(functools.partial(react_kernel, group=min(128, blocks), sl...  14.6 us
    ppermute x4, waiting for transfers between devices, from_partner(): return lax.ppermute(values, 'yz', [(i, i ^ mask) for i in range(count)])  11.2 us
    pallas_call x1, Pallas kernels, moments(): pl.pallas_call(functools.partial(moments_kernel, high=high, rows=rows), o...  7.05 us
    ppermute x4, starting transfers between devices, from_partner(): return lax.ppermute(values, 'yz', [(i, i ^ mask) for i in range(count)])  6.21 us
    ppermute x2, starting transfers between devices, swap_pairs(): near = lax.ppermute(near, 'gx', first)  3.67 us
    ppermute x3, starting transfers between devices, local(): lax.ppermute(batch_inverse, 'gx', [(i, i ^ distance) for i in range(slabs)])  3.11 us
    ppermute x2, starting transfers between devices, swap_pairs(): far = lax.ppermute(far, 'gx', second)  1.32 us
  transfers between devices with their start and end apart: 11, of which 4 were waited for; matrix products, arithmetic and copies ran while one was open for 6% of the time, Pallas kernels for 14%

profile of v1, /device:TPU:0, one launch (start us, length us, event | category | flops | bytes accessed | tf_op | source)
XLA Modules:
  0.0 51.9 jit_solution(8642002478206327586)
XLA Ops:
  0.0 3.0 %collective-permute-start.3 = (f32[1,20,20]{2,0,1:T(1,128)}, f32[1,20,20]{2,0,1:T(1,128)S(1)}, u32[]{:S(2)}, u32[]{:S(2)}) collective-permute-start(f32[1,20,20]{2,0,1:T(1,128)} %param.15), channel_id=1, source_target_pairs={{0,16},{8,24},{16,0},{24,8},{1,17},{9,25},{17,1},{25,9},{2,18},{10... | collective-permute-start | bytes 4808 | tf_op jit(solution)/shard_map/ppermute | solution.py:321
  3.0 0.1 collective-permute-start.4
  3.1 0.1 pad_add_fusion.place_ref
  3.2 7.1 %moments.1 = f32[3,168,128]{2,1,0:T(8,128)S(1)} custom-call(s32[3]{0:T(128)S(1)} %pad_add_fusion.place_ref, f32[20,128,128]{2,1,0:T(8,128)} %bitcast.27, f32[128,128]{1,0:T(8,128)} %mass_ref.1, s32[128,128]{1,0:T(8,128)} %cell_ref.3), custom_call_target="tpu_custom_call" | custom-call | flops 4831838208 | bytes 1310720 | tf_op jit(solution)/shard_map/moments/pallas_call | solution.py:85
  10.3 0.5 collective-permute-start
  10.7 0.7 %collective-permute-start.1 = (f32[168,128]{1,0:T(8,128)S(1)}, f32[168,128]{1,0:T(8,128)S(1)}, u32[]{:S(2)}, u32[]{:S(2)}) collective-permute-start(f32[168,128]{1,0:T(8,128)S(1)} %get-tuple-element.12), channel_id=1, source_target_pairs={{8,16},{16,8},{9,17},{17,9},{10,18},{18,10},{11,19},{19,11},{12,20... | collective-permute-start | bytes 258056 | tf_op jit(solution)/shard_map/ppermute | solution.py:300
  11.4 0.1 select_reduce_fusion
  11.5 0.1 select_reduce_fusion.1
  11.7 0.6 %fusion.14 = (s32[]{:T(128)}, s32[]{:T(128)}) fusion(s32[128]{0:T(128)S(1)} %copy-done.7), kind=kLoop, calls=%fused_computation.55 | loop fusion | flops 254 | bytes 520 | tf_op jit(solution)/shard_map/reduce_sum | solution.py:275
  13.0 0.1 copy.20
  13.1 0.1 pad_maximum_fusion.2
  13.2 0.1 reshape.19
  13.4 2.7 %collective-permute-start.7 = (f32[184,128]{1,0:T(8,128)S(1)}, f32[184,128]{1,0:T(8,128)S(1)}, u32[]{:S(2)}, u32[]{:S(2)}) collective-permute-start(f32[184,128]{1,0:T(8,128)S(1)} %pad_maximum_fusion.1), channel_id=1, source_target_pairs={{0,3},{1,2},{2,1},{3,0},{4,7},{5,6},{6,5},{7,4},{8,11},{9,10},{10,... | collective-permute-start | bytes 282632 | tf_op jit(solution)/shard_map/ppermute | solution.py:291
  16.1 0.4 collective-permute-start.6
  16.5 0.4 collective-permute-start.5
  17.0 2.0 %collective-permute-done.7 = f32[184,128]{1,0:T(8,128)S(1)} collective-permute-done((f32[184,128]{1,0:T(8,128)S(1)}, f32[184,128]{1,0:T(8,128)S(1)}, u32[]{:S(2)}, u32[]{:S(2)}) %collective-permute-start.7) | collective-permute-done | bytes 94240 | tf_op jit(solution)/shard_map/ppermute | solution.py:291
  18.9 1.7 %collective-permute-done.6 = f32[184,128]{1,0:T(8,128)S(1)} collective-permute-done((f32[184,128]{1,0:T(8,128)S(1)}, f32[184,128]{1,0:T(8,128)S(1)}, u32[]{:S(2)}, u32[]{:S(2)}) %collective-permute-start.6) | collective-permute-done | bytes 94240 | tf_op jit(solution)/shard_map/ppermute | solution.py:291
  20.7 1.5 %collective-permute-done.5 = f32[184,128]{1,0:T(8,128)S(1)} collective-permute-done((f32[184,128]{1,0:T(8,128)S(1)}, f32[184,128]{1,0:T(8,128)S(1)}, u32[]{:S(2)}, u32[]{:S(2)}) %collective-permute-start.5) | collective-permute-done | bytes 94240 | tf_op jit(solution)/shard_map/ppermute | solution.py:291
  22.2 2.7 %collective-permute-start.8 = (f32[232,128]{1,0:T(8,128)S(1)}, f32[232,128]{1,0:T(8,128)S(1)}, u32[]{:S(2)}, u32[]{:S(2)}) collective-permute-start(f32[232,128]{1,0:T(8,128)S(1)} %get-tuple-element.14), channel_id=1, source_target_pairs={{0,4},{1,5},{2,6},{3,7},{4,0},{5,1},{6,2},{7,3},{8,12},{9,13},{10,... | collective-permute-start | bytes 356360 | tf_op jit(solution)/shard_map/ppermute | solution.py:291
  24.9 0.1 slice.72
  25.5 0.1 concatenate.36.rates_ref
  25.6 0.1 convert_reduce_fusion.sched_ref
  25.8 6.0 %collective-permute-done.8 = f32[232,128]{1,0:T(8,128)S(1)} collective-permute-done((f32[232,128]{1,0:T(8,128)S(1)}, f32[232,128]{1,0:T(8,128)S(1)}, u32[]{:S(2)}, u32[]{:S(2)}) %collective-permute-start.8) | collective-permute-done | bytes 118816 | tf_op jit(solution)/shard_map/ppermute | solution.py:291
  31.8 0.7 %collective-permute-start.10 = (f32[168,128]{1,0:T(8,128)S(1)}, f32[168,128]{1,0:T(8,128)S(1)}, u32[]{:S(2)}, u32[]{:S(2)}) collective-permute-start(f32[168,128]{1,0:T(8,128)S(1)} %slice_add_fusion.own_ref), channel_id=1, source_target_pairs={{8,16},{16,8},{9,17},{17,9},{10,18},{18,10},{11,19},{19,11},{12,20... | collective-permute-start | bytes 258056 | tf_op jit(solution)/shard_map/ppermute | solution.py:300
  32.5 3.2 %collective-permute-start.9 = (f32[168,128]{1,0:T(8,128)S(1)}, f32[168,128]{1,0:T(8,128)S(1)}, u32[]{:S(2)}, u32[]{:S(2)}) collective-permute-start(f32[168,128]{1,0:T(8,128)S(1)} %slice_add_fusion.own_ref), channel_id=1, source_target_pairs={{0,8},{8,0},{16,24},{24,16},{1,9},{9,1},{17,25},{25,17},{2,10},{10... | collective-permute-start | bytes 258056 | tf_op jit(solution)/shard_map/ppermute | solution.py:299
  35.7 0.1 copy.26
  35.9 0.0 copy-start.1
  36.0 0.0 copy-start.2
  36.0 0.2 copy.24
  36.2 0.8 %reduce-precision_convert_fusion = (bf16[32,24,88]{2,1,0:T(8,128)(2,1)S(1)}, bf16[32,24,88]{2,1,0:T(8,128)(2,1)S(1)}) fusion(f32[32,24,20]{1,2,0:T(8,128)S(1)} %copy.24, f32[20,84]{1,0:T(8,128)S(1)} %copy-done.4), kind=kOutput, calls=%fused_computation.4 | convolution fusion | flops 16558080 | bytes 338496 | tf_op jit(solution)/shard_map/qij,jr->qir/dot_general | solution.py:263
  37.0 0.2 fusion.1.net_ref
  37.3 14.6 %react.1 = f32[20,128,128]{2,1,0:T(8,128)} custom-call(s32[1]{0:T(128)} %bitcast.length_ref, s32[896]{0:T(1024)S(1)} %convert_reduce_fusion.sched_ref, s32[256]{0:T(256)S(1)} %pad.18.batch_ref, s32[3]{0:T(128)S(1)} %pad_add_fusion.place_ref, f32[168,128]{1,0:T(8,128)S(1)} %slice_add_fusion.own_ref, f32[168,128]{1,0:T(8,128)S(1)} %collective-permute-done.9.near_ref, ...), custom_call_target="tpu_custom_call" | custom-call | flops 4831838208 | bytes 2621440 | tf_op jit(solution)/shard_map/react/pallas_call | solution.py:223
  (43 shorter events, 0.3 us)
Async XLA Ops:
  0.0 13.1 %collective-permute-start.3 = (f32[1,20,20]{2,0,1:T(1,128)}, f32[1,20,20]{2,0,1:T(1,128)S(1)}, u32[]{:S(2)}, u32[]{:S(2)}) collective-permute-start(f32[1,20,20]{2,0,1:T(1,128)} %param.15), channel_id=1, source_target_pairs={{0,16},{8,24},{16,0},{24,8},{1,17},{9,25},{17,1},{25,9},{2,18},{10... | collective-permute-start | bytes 4808 | tf_op jit(solution)/shard_map/ppermute | solution.py:321
  3.0 10.1 %collective-permute-start.2 = (f32[1,20,20]{2,0,1:T(1,128)}, f32[1,20,20]{2,0,1:T(1,128)S(1)}, u32[]{:S(2)}, u32[]{:S(2)}) collective-permute-start(f32[1,20,20]{2,0,1:T(1,128)} %param.15), channel_id=1, source_target_pairs={{0,8},{8,0},{16,24},{24,16},{1,9},{9,1},{17,25},{25,17},{2,10},{10... | collective-permute-start | bytes 4808 | tf_op jit(solution)/shard_map/ppermute | solution.py:321
  3.0 10.1 %collective-permute-start.4 = (f32[1,20,20]{2,0,1:T(1,128)}, f32[1,20,20]{2,0,1:T(1,128)S(1)}, u32[]{:S(2)}, u32[]{:S(2)}) collective-permute-start(f32[1,20,20]{2,0,1:T(1,128)} %param.15), channel_id=1, source_target_pairs={{0,24},{8,16},{16,8},{24,0},{1,25},{9,17},{17,9},{25,1},{2,26},{10... | collective-permute-start | bytes 4808 | tf_op jit(solution)/shard_map/ppermute | solution.py:321
  3.2 8.2 %copy-start.6 = (s32[1,128]{1,0:T(1,128)S(1)}, s32[1,128]{1,0:T(1,128)}, u32[]{:S(2)}) copy-start(s32[1,128]{1,0:T(1,128)} %param.14) | copy-start | bytes 1540
  3.2 8.3 %copy-start.7 = (s32[128]{0:T(128)S(1)}, s32[128]{0:T(128)}, u32[]{:S(2)}) copy-start(s32[128]{0:T(128)} %param.13) | copy-start | bytes 1540
  3.2 9.8 %copy-start.3 = (f32[84,20]{0,1:T(8,128)S(1)}, f32[84,20]{0,1:T(8,128)}, u32[]{:S(2)}) copy-start(f32[84,20]{0,1:T(8,128)} %param.16) | copy-start | bytes 20164
  3.2 9.9 %copy-start.5 = (f32[1,20,20]{2,0,1:T(1,128)S(1)}, f32[1,20,20]{2,0,1:T(1,128)}, u32[]{:S(2)}) copy-start(f32[1,20,20]{2,0,1:T(1,128)} %param.15) | copy-start | bytes 4804
  10.3 3.0 %collective-permute-start = (f32[168,128]{1,0:T(8,128)S(1)}, f32[168,128]{1,0:T(8,128)S(1)}, u32[]{:S(2)}, u32[]{:S(2)}) collective-permute-start(f32[168,128]{1,0:T(8,128)S(1)} %get-tuple-element.11), channel_id=1, source_target_pairs={{0,8},{8,0},{16,24},{24,16},{1,9},{9,1},{17,25},{25,17},{2,10},{10... | collective-permute-start | bytes 258056 | tf_op jit(solution)/shard_map/ppermute | solution.py:299
  10.7 2.6 %collective-permute-start.1 = (f32[168,128]{1,0:T(8,128)S(1)}, f32[168,128]{1,0:T(8,128)S(1)}, u32[]{:S(2)}, u32[]{:S(2)}) collective-permute-start(f32[168,128]{1,0:T(8,128)S(1)} %get-tuple-element.12), channel_id=1, source_target_pairs={{8,16},{16,8},{9,17},{17,9},{10,18},{18,10},{11,19},{19,11},{12,20... | collective-permute-start | bytes 258056 | tf_op jit(solution)/shard_map/ppermute | solution.py:300
  13.4 5.5 %collective-permute-start.7 = (f32[184,128]{1,0:T(8,128)S(1)}, f32[184,128]{1,0:T(8,128)S(1)}, u32[]{:S(2)}, u32[]{:S(2)}) collective-permute-start(f32[184,128]{1,0:T(8,128)S(1)} %pad_maximum_fusion.1), channel_id=1, source_target_pairs={{0,3},{1,2},{2,1},{3,0},{4,7},{5,6},{6,5},{7,4},{8,11},{9,10},{10,... | collective-permute-start | bytes 282632 | tf_op jit(solution)/shard_map/ppermute | solution.py:291
  16.1 4.6 %collective-permute-start.6 = (f32[184,128]{1,0:T(8,128)S(1)}, f32[184,128]{1,0:T(8,128)S(1)}, u32[]{:S(2)}, u32[]{:S(2)}) collective-permute-start(f32[184,128]{1,0:T(8,128)S(1)} %pad_maximum_fusion.1), channel_id=1, source_target_pairs={{0,2},{1,3},{2,0},{3,1},{4,6},{5,7},{6,4},{7,5},{8,10},{9,11},{10,... | collective-permute-start | bytes 282632 | tf_op jit(solution)/shard_map/ppermute | solution.py:291
  16.5 5.6 %collective-permute-start.5 = (f32[184,128]{1,0:T(8,128)S(1)}, f32[184,128]{1,0:T(8,128)S(1)}, u32[]{:S(2)}, u32[]{:S(2)}) collective-permute-start(f32[184,128]{1,0:T(8,128)S(1)} %pad_maximum_fusion.1), channel_id=1, source_target_pairs={{0,1},{1,0},{2,3},{3,2},{4,5},{5,4},{6,7},{7,6},{8,9},{9,8},{10,11... | collective-permute-start | bytes 282632 | tf_op jit(solution)/shard_map/ppermute | solution.py:291
  22.2 9.6 %collective-permute-start.8 = (f32[232,128]{1,0:T(8,128)S(1)}, f32[232,128]{1,0:T(8,128)S(1)}, u32[]{:S(2)}, u32[]{:S(2)}) collective-permute-start(f32[232,128]{1,0:T(8,128)S(1)} %get-tuple-element.14), channel_id=1, source_target_pairs={{0,4},{1,5},{2,6},{3,7},{4,0},{5,1},{6,2},{7,3},{8,12},{9,13},{10,... | collective-permute-start | bytes 356360 | tf_op jit(solution)/shard_map/ppermute | solution.py:291
  25.6 10.5 %copy-start.4 = (f32[20,84]{1,0:T(8,128)S(1)}, f32[20,84]{1,0:T(8,128)}, u32[]{:S(2)}) copy-start(f32[20,84]{1,0:T(8,128)} %param.17) | copy-start | bytes 20164
  31.8 5.4 %collective-permute-start.10 = (f32[168,128]{1,0:T(8,128)S(1)}, f32[168,128]{1,0:T(8,128)S(1)}, u32[]{:S(2)}, u32[]{:S(2)}) collective-permute-start(f32[168,128]{1,0:T(8,128)S(1)} %slice_add_fusion.own_ref), channel_id=1, source_target_pairs={{8,16},{16,8},{9,17},{17,9},{10,18},{18,10},{11,19},{19,11},{12,20... | collective-permute-start | bytes 258056 | tf_op jit(solution)/shard_map/ppermute | solution.py:300
  32.5 4.7 %collective-permute-start.9 = (f32[168,128]{1,0:T(8,128)S(1)}, f32[168,128]{1,0:T(8,128)S(1)}, u32[]{:S(2)}, u32[]{:S(2)}) collective-permute-start(f32[168,128]{1,0:T(8,128)S(1)} %slice_add_fusion.own_ref), channel_id=1, source_target_pairs={{0,8},{8,0},{16,24},{24,16},{1,9},{9,1},{17,25},{25,17},{2,10},{10... | collective-permute-start | bytes 258056 | tf_op jit(solution)/shard_map/ppermute | solution.py:299
  35.9 1.3 %copy-start = (f32[128,20,128]{2,0,1:T(8,128)S(1)}, f32[128,20,128]{2,0,1:T(8,128)}, u32[]{:S(2)}) copy-start(f32[128,20,128]{2,0,1:T(8,128)} %param.9) | copy-start | bytes 3932164
  35.9 1.3 %copy-start.1 = (s32[128,128]{1,0:T(8,128)S(1)}, s32[128,128]{1,0:T(8,128)}, u32[]{:S(2)}) copy-start(s32[128,128]{1,0:T(8,128)} %cell_ref.3) | copy-start | bytes 196612
  36.0 1.3 %copy-start.2 = (f32[128,128]{1,0:T(8,128)S(1)}, f32[128,128]{1,0:T(8,128)}, u32[]{:S(2)}) copy-start(f32[128,128]{1,0:T(8,128)} %rate_ref.1) | copy-start | bytes 196612

commit v2 on v1

--- a/solution.py
+++ b/solution.py
@@ -221,7 +221,7 @@
     high = 3 * (own.shape[0] * lanes // (species + 1)) // LOW
     vmem = pl.BlockSpec(memory_space=pltpu.VMEM)
     return pl.pallas_call(
-        functools.partial(react_kernel, group=min(128, blocks), slots=slots, chunk=8),
+        functools.partial(react_kernel, group=min(128, blocks), slots=slots, chunk=4),
         out_shape=jax.ShapeDtypeStruct(comp.shape, F32),
         grid_spec=pltpu.PrefetchScalarGridSpec(
             num_scalar_prefetch=4,
@@ -316,15 +316,16 @@
     odd = slab % 2
     place = jnp.stack([(slab - 1) * slab_cells, 2 - odd, 1 + odd]).astype(jnp.int32)
 
-    inverses = [batch_inverse]
-    for distance in range(1, slabs):
-        inverses.append(lax.ppermute(batch_inverse, "gx", [(i, i ^ distance) for i in range(slabs)]))
-    bits = [1 << k for k in range((columns - 1).bit_length())]
     comp = jnp.transpose(composition, (1, 0, 2))
     held = [pltpu.with_memory_space_constraint(v, pltpu.HBM) for v in (comp, particle_mass, cell_index)]
     partial = moments(place, *held, slab_cells, rows)
     near, far = partial[1], partial[2]
+    near, far, own_inverse = lax.optimization_barrier((near, far, batch_inverse))
     got_near, got_far = swap_pairs(near, far)
+    inverses = [own_inverse]
+    for distance in range(1, slabs):
+        inverses.append(lax.ppermute(own_inverse, "gx", [(i, i ^ distance) for i in range(slabs)]))
+    bits = [1 << k for k in range((columns - 1).bit_length())]
     inverses = flat_inverses(jnp.concatenate(inverses, axis=0), lanes)
     own = partial[0] + got_near + got_far
     sums = own.shape[0]

time: 52.1 us -> 51.9 us (level)
  transfers between devices with their start and end apart: 11 -> 11, of which waited for: 4 -> 5; matrix products, arithmetic and copies ran while one was open for 6% -> 6% of each run, Pallas kernels for 14% -> 0%
where the time goes in v2:
time: 51.9 us; the launch traced here: 51.7 us
  Pallas kernels  21.6 us (42%)
  starting transfers between devices  14.2 us (27%)
  waiting for transfers between devices  11.1 us (21%)
  between operations  1.59 us (3%)
  other arithmetic  1.43 us (3%)
  local copies, waits for them, and re-layouts  0.87 us (2%)
  matrix products  0.8 us (2%)
    pallas_call x1, Pallas kernels, react(): pl.pallas_call(functools.partial(react_kernel, group=min(128, blocks), sl...  14.6 us
    ppermute x4, waiting for transfers between devices, from_partner(): return lax.ppermute(values, 'yz', [(i, i ^ mask) for i in range(count)])  10.9 us
    pallas_call x1, Pallas kernels, moments(): pl.pallas_call(functools.partial(moments_kernel, high=high, rows=rows), o...  7.05 us
    ppermute x4, starting transfers between devices, from_partner(): return lax.ppermute(values, 'yz', [(i, i ^ mask) for i in range(count)])  6.21 us
    ppermute x2, starting transfers between devices, swap_pairs(): near = lax.ppermute(near, 'gx', first)  3.53 us
    ppermute x3, starting transfers between devices, local(): lax.ppermute(own_inverse, 'gx', [(i, i ^ distance) for i in range(slabs)])  3.18 us
    ppermute x2, starting transfers between devices, swap_pairs(): far = lax.ppermute(far, 'gx', second)  1.32 us
  transfers between devices with their start and end apart: 11, of which 5 were waited for; matrix products, arithmetic and copies ran while one was open for 6% of the time, Pallas kernels for 0%

profile of v2, /device:TPU:0, one launch (start us, length us, event | category | flops | bytes accessed | tf_op | source)
XLA Modules:
  0.0 51.7 jit_solution(13823017490672392942)
XLA Ops:
  0.0 0.1 pad_add_fusion.place_ref
  0.1 7.0 %moments.1 = f32[3,168,128]{2,1,0:T(8,128)S(1)} custom-call(s32[3]{0:T(128)S(1)} %pad_add_fusion.place_ref, f32[20,128,128]{2,1,0:T(8,128)} %bitcast.27, f32[128,128]{1,0:T(8,128)} %mass_ref.1, s32[128,128]{1,0:T(8,128)} %cell_ref.3), custom_call_target="tpu_custom_call" | custom-call | flops 4831838208 | bytes 1310720 | tf_op jit(solution)/shard_map/moments/pallas_call | solution.py:85
  7.2 2.5 %collective-permute-start.4 = (f32[1,20,20]{2,0,1:T(1,128)S(1)}, f32[1,20,20]{2,0,1:T(1,128)S(1)}, u32[]{:S(2)}, u32[]{:S(2)}) collective-permute-start(f32[1,20,20]{2,0,1:T(1,128)S(1)} %copy-done.5), channel_id=1, source_target_pairs={{0,24},{8,16},{16,8},{24,0},{1,25},{9,17},{17,9},{25,1},{2,26},{10... | collective-permute-start | bytes 4808 | tf_op jit(solution)/shard_map/ppermute | solution.py:327
  9.7 0.6 %collective-permute-start.3 = (f32[1,20,20]{2,0,1:T(1,128)S(1)}, f32[1,20,20]{2,0,1:T(1,128)S(1)}, u32[]{:S(2)}, u32[]{:S(2)}) collective-permute-start(f32[1,20,20]{2,0,1:T(1,128)S(1)} %copy-done.5), channel_id=1, source_target_pairs={{0,16},{8,24},{16,0},{24,8},{1,17},{9,25},{17,1},{25,9},{2,18},{10... | collective-permute-start | bytes 4808 | tf_op jit(solution)/shard_map/ppermute | solution.py:327
  10.3 0.0 collective-permute-start.2
  10.4 0.5 collective-permute-start
  10.8 0.7 %collective-permute-start.1 = (f32[168,128]{1,0:T(8,128)S(1)}, f32[168,128]{1,0:T(8,128)S(1)}, u32[]{:S(2)}, u32[]{:S(2)}) collective-permute-start(f32[168,128]{1,0:T(8,128)S(1)} %get-tuple-element.9), channel_id=1, source_target_pairs={{8,16},{16,8},{9,17},{17,9},{10,18},{18,10},{11,19},{19,11},{12,20... | collective-permute-start | bytes 258056 | tf_op jit(solution)/shard_map/ppermute | solution.py:300
  11.5 0.1 select_reduce_fusion
  11.6 0.1 select_reduce_fusion.1
  11.7 0.6 %fusion.14 = (s32[]{:T(128)}, s32[]{:T(128)}) fusion(s32[128]{0:T(128)S(1)} %copy-done.7), kind=kLoop, calls=%fused_computation.55 | loop fusion | flops 254 | bytes 520 | tf_op jit(solution)/shard_map/reduce_sum | solution.py:275
  13.1 0.1 copy.20
  13.2 0.2 collective-permute-done.3
  13.4 0.1 pad_maximum_fusion.2
  13.4 0.1 reshape.19
  13.6 2.6 %collective-permute-start.7 = (f32[184,128]{1,0:T(8,128)S(1)}, f32[184,128]{1,0:T(8,128)S(1)}, u32[]{:S(2)}, u32[]{:S(2)}) collective-permute-start(f32[184,128]{1,0:T(8,128)S(1)} %pad_maximum_fusion.1), channel_id=1, source_target_pairs={{0,3},{1,2},{2,1},{3,0},{4,7},{5,6},{6,5},{7,4},{8,11},{9,10},{10,... | collective-permute-start | bytes 282632 | tf_op jit(solution)/shard_map/ppermute | solution.py:291
  16.2 0.5 collective-permute-start.6
  16.6 0.5 %collective-permute-start.5 = (f32[184,128]{1,0:T(8,128)S(1)}, f32[184,128]{1,0:T(8,128)S(1)}, u32[]{:S(2)}, u32[]{:S(2)}) collective-permute-start(f32[184,128]{1,0:T(8,128)S(1)} %pad_maximum_fusion.1), channel_id=1, source_target_pairs={{0,1},{1,0},{2,3},{3,2},{4,5},{5,4},{6,7},{7,6},{8,9},{9,8},{10,11... | collective-permute-start | bytes 282632 | tf_op jit(solution)/shard_map/ppermute | solution.py:291
  17.2 2.0 %collective-permute-done.7 = f32[184,128]{1,0:T(8,128)S(1)} collective-permute-done((f32[184,128]{1,0:T(8,128)S(1)}, f32[184,128]{1,0:T(8,128)S(1)}, u32[]{:S(2)}, u32[]{:S(2)}) %collective-permute-start.7) | collective-permute-done | bytes 94240 | tf_op jit(solution)/shard_map/ppermute | solution.py:291
  19.1 1.8 %collective-permute-done.6 = f32[184,128]{1,0:T(8,128)S(1)} collective-permute-done((f32[184,128]{1,0:T(8,128)S(1)}, f32[184,128]{1,0:T(8,128)S(1)}, u32[]{:S(2)}, u32[]{:S(2)}) %collective-permute-start.6) | collective-permute-done | bytes 94240 | tf_op jit(solution)/shard_map/ppermute | solution.py:291
  21.0 1.5 %collective-permute-done.5 = f32[184,128]{1,0:T(8,128)S(1)} collective-permute-done((f32[184,128]{1,0:T(8,128)S(1)}, f32[184,128]{1,0:T(8,128)S(1)}, u32[]{:S(2)}, u32[]{:S(2)}) %collective-permute-start.5) | collective-permute-done | bytes 94240 | tf_op jit(solution)/shard_map/ppermute | solution.py:291
  22.5 2.7 %collective-permute-start.8 = (f32[232,128]{1,0:T(8,128)S(1)}, f32[232,128]{1,0:T(8,128)S(1)}, u32[]{:S(2)}, u32[]{:S(2)}) collective-permute-start(f32[232,128]{1,0:T(8,128)S(1)} %get-tuple-element.20), channel_id=1, source_target_pairs={{0,4},{1,5},{2,6},{3,7},{4,0},{5,1},{6,2},{7,3},{8,12},{9,13},{10,... | collective-permute-start | bytes 356360 | tf_op jit(solution)/shard_map/ppermute | solution.py:291
  25.2 0.1 slice.72
  25.8 0.1 concatenate.36.rates_ref
  26.0 0.1 convert_reduce_fusion.sched_ref
  26.1 5.7 %collective-permute-done.8 = f32[232,128]{1,0:T(8,128)S(1)} collective-permute-done((f32[232,128]{1,0:T(8,128)S(1)}, f32[232,128]{1,0:T(8,128)S(1)}, u32[]{:S(2)}, u32[]{:S(2)}) %collective-permute-start.8) | collective-permute-done | bytes 118816 | tf_op jit(solution)/shard_map/ppermute | solution.py:291
  31.8 0.7 %collective-permute-start.10 = (f32[168,128]{1,0:T(8,128)S(1)}, f32[168,128]{1,0:T(8,128)S(1)}, u32[]{:S(2)}, u32[]{:S(2)}) collective-permute-start(f32[168,128]{1,0:T(8,128)S(1)} %slice_add_fusion.own_ref), channel_id=1, source_target_pairs={{8,16},{16,8},{9,17},{17,9},{10,18},{18,10},{11,19},{19,11},{12,20... | collective-permute-start | bytes 258056 | tf_op jit(solution)/shard_map/ppermute | solution.py:300
  32.5 3.1 %collective-permute-start.9 = (f32[168,128]{1,0:T(8,128)S(1)}, f32[168,128]{1,0:T(8,128)S(1)}, u32[]{:S(2)}, u32[]{:S(2)}) collective-permute-start(f32[168,128]{1,0:T(8,128)S(1)} %slice_add_fusion.own_ref), channel_id=1, source_target_pairs={{0,8},{8,0},{16,24},{24,16},{1,9},{9,1},{17,25},{25,17},{2,10},{10... | collective-permute-start | bytes 258056 | tf_op jit(solution)/shard_map/ppermute | solution.py:299
  35.5 0.1 copy.26
  35.8 0.2 copy.24
  36.0 0.8 %reduce-precision_convert_fusion = (bf16[32,24,88]{2,1,0:T(8,128)(2,1)S(1)}, bf16[32,24,88]{2,1,0:T(8,128)(2,1)S(1)}) fusion(f32[32,24,20]{1,2,0:T(8,128)S(1)} %copy.24, f32[20,84]{1,0:T(8,128)S(1)} %copy-done.4), kind=kOutput, calls=%fused_computation.4 | convolution fusion | flops 16558080 | bytes 338496 | tf_op jit(solution)/shard_map/qij,jr->qir/dot_general | solution.py:263
  36.8 0.2 fusion.1.net_ref
  37.1 14.6 %react.1 = f32[20,128,128]{2,1,0:T(8,128)} custom-call(s32[1]{0:T(128)} %bitcast.length_ref, s32[896]{0:T(1024)S(1)} %convert_reduce_fusion.sched_ref, s32[256]{0:T(256)S(1)} %pad.18.batch_ref, s32[3]{0:T(128)S(1)} %pad_add_fusion.place_ref, f32[168,128]{1,0:T(8,128)S(1)} %slice_add_fusion.own_ref, f32[168,128]{1,0:T(8,128)S(1)} %collective-permute-done.9.near_ref, ...), custom_call_target="tpu_custom_call" | custom-call | flops 4831838208 | bytes 2621440 | tf_op jit(solution)/shard_map/react/pallas_call | solution.py:223
  (43 shorter events, 0.3 us)
Async XLA Ops:
  0.1 7.1 %copy-start.5 = (f32[1,20,20]{2,0,1:T(1,128)S(1)}, f32[1,20,20]{2,0,1:T(1,128)}, u32[]{:S(2)}) copy-start(f32[1,20,20]{2,0,1:T(1,128)} %param.15) | copy-start | bytes 4804
  0.1 11.4 %copy-start.6 = (s32[1,128]{1,0:T(1,128)S(1)}, s32[1,128]{1,0:T(1,128)}, u32[]{:S(2)}) copy-start(s32[1,128]{1,0:T(1,128)} %param.14) | copy-start | bytes 1540
  0.1 11.5 %copy-start.7 = (s32[128]{0:T(128)S(1)}, s32[128]{0:T(128)}, u32[]{:S(2)}) copy-start(s32[128]{0:T(128)} %param.13) | copy-start | bytes 1540
  0.1 13.0 %copy-start.3 = (f32[84,20]{0,1:T(8,128)S(1)}, f32[84,20]{0,1:T(8,128)}, u32[]{:S(2)}) copy-start(f32[84,20]{0,1:T(8,128)} %param.16) | copy-start | bytes 20164
  7.2 6.0 %collective-permute-start.4 = (f32[1,20,20]{2,0,1:T(1,128)S(1)}, f32[1,20,20]{2,0,1:T(1,128)S(1)}, u32[]{:S(2)}, u32[]{:S(2)}) collective-permute-start(f32[1,20,20]{2,0,1:T(1,128)S(1)} %copy-done.5), channel_id=1, source_target_pairs={{0,24},{8,16},{16,8},{24,0},{1,25},{9,17},{17,9},{25,1},{2,26},{10... | collective-permute-start | bytes 4808 | tf_op jit(solution)/shard_map/ppermute | solution.py:327
  9.7 3.7 %collective-permute-start.3 = (f32[1,20,20]{2,0,1:T(1,128)S(1)}, f32[1,20,20]{2,0,1:T(1,128)S(1)}, u32[]{:S(2)}, u32[]{:S(2)}) collective-permute-start(f32[1,20,20]{2,0,1:T(1,128)S(1)} %copy-done.5), channel_id=1, source_target_pairs={{0,16},{8,24},{16,0},{24,8},{1,17},{9,25},{17,1},{25,9},{2,18},{10... | collective-permute-start | bytes 4808 | tf_op jit(solution)/shard_map/ppermute | solution.py:327
  10.3 3.0 %collective-permute-start.2 = (f32[1,20,20]{2,0,1:T(1,128)S(1)}, f32[1,20,20]{2,0,1:T(1,128)S(1)}, u32[]{:S(2)}, u32[]{:S(2)}) collective-permute-start(f32[1,20,20]{2,0,1:T(1,128)S(1)} %copy-done.5), channel_id=1, source_target_pairs={{0,8},{8,0},{16,24},{24,16},{1,9},{9,1},{17,25},{25,17},{2,10},{10... | collective-permute-start | bytes 4808 | tf_op jit(solution)/shard_map/ppermute | solution.py:327
  10.4 3.2 %collective-permute-start = (f32[168,128]{1,0:T(8,128)S(1)}, f32[168,128]{1,0:T(8,128)S(1)}, u32[]{:S(2)}, u32[]{:S(2)}) collective-permute-start(f32[168,128]{1,0:T(8,128)S(1)} %get-tuple-element.8), channel_id=1, source_target_pairs={{0,8},{8,0},{16,24},{24,16},{1,9},{9,1},{17,25},{25,17},{2,10},{10... | collective-permute-start | bytes 258056 | tf_op jit(solution)/shard_map/ppermute | solution.py:299
  10.8 2.7 %collective-permute-start.1 = (f32[168,128]{1,0:T(8,128)S(1)}, f32[168,128]{1,0:T(8,128)S(1)}, u32[]{:S(2)}, u32[]{:S(2)}) collective-permute-start(f32[168,128]{1,0:T(8,128)S(1)} %get-tuple-element.9), channel_id=1, source_target_pairs={{8,16},{16,8},{9,17},{17,9},{10,18},{18,10},{11,19},{19,11},{12,20... | collective-permute-start | bytes 258056 | tf_op jit(solution)/shard_map/ppermute | solution.py:300
  13.6 5.5 %collective-permute-start.7 = (f32[184,128]{1,0:T(8,128)S(1)}, f32[184,128]{1,0:T(8,128)S(1)}, u32[]{:S(2)}, u32[]{:S(2)}) collective-permute-start(f32[184,128]{1,0:T(8,128)S(1)} %pad_maximum_fusion.1), channel_id=1, source_target_pairs={{0,3},{1,2},{2,1},{3,0},{4,7},{5,6},{6,5},{7,4},{8,11},{9,10},{10,... | collective-permute-start | bytes 282632 | tf_op jit(solution)/shard_map/ppermute | solution.py:291
  16.2 4.8 %collective-permute-start.6 = (f32[184,128]{1,0:T(8,128)S(1)}, f32[184,128]{1,0:T(8,128)S(1)}, u32[]{:S(2)}, u32[]{:S(2)}) collective-permute-start(f32[184,128]{1,0:T(8,128)S(1)} %pad_maximum_fusion.1), channel_id=1, source_target_pairs={{0,2},{1,3},{2,0},{3,1},{4,6},{5,7},{6,4},{7,5},{8,10},{9,11},{10,... | collective-permute-start | bytes 282632 | tf_op jit(solution)/shard_map/ppermute | solution.py:291
  16.6 5.8 %collective-permute-start.5 = (f32[184,128]{1,0:T(8,128)S(1)}, f32[184,128]{1,0:T(8,128)S(1)}, u32[]{:S(2)}, u32[]{:S(2)}) collective-permute-start(f32[184,128]{1,0:T(8,128)S(1)} %pad_maximum_fusion.1), channel_id=1, source_target_pairs={{0,1},{1,0},{2,3},{3,2},{4,5},{5,4},{6,7},{7,6},{8,9},{9,8},{10,11... | collective-permute-start | bytes 282632 | tf_op jit(solution)/shard_map/ppermute | solution.py:291
  22.5 9.2 %collective-permute-start.8 = (f32[232,128]{1,0:T(8,128)S(1)}, f32[232,128]{1,0:T(8,128)S(1)}, u32[]{:S(2)}, u32[]{:S(2)}) collective-permute-start(f32[232,128]{1,0:T(8,128)S(1)} %get-tuple-element.20), channel_id=1, source_target_pairs={{0,4},{1,5},{2,6},{3,7},{4,0},{5,1},{6,2},{7,3},{8,12},{9,13},{10,... | collective-permute-start | bytes 356360 | tf_op jit(solution)/shard_map/ppermute | solution.py:291
  26.0 10.0 %copy-start.4 = (f32[20,84]{1,0:T(8,128)S(1)}, f32[20,84]{1,0:T(8,128)}, u32[]{:S(2)}) copy-start(f32[20,84]{1,0:T(8,128)} %param.17) | copy-start | bytes 20164
  31.8 5.3 %collective-permute-start.10 = (f32[168,128]{1,0:T(8,128)S(1)}, f32[168,128]{1,0:T(8,128)S(1)}, u32[]{:S(2)}, u32[]{:S(2)}) collective-permute-start(f32[168,128]{1,0:T(8,128)S(1)} %slice_add_fusion.own_ref), channel_id=1, source_target_pairs={{8,16},{16,8},{9,17},{17,9},{10,18},{18,10},{11,19},{19,11},{12,20... | collective-permute-start | bytes 258056 | tf_op jit(solution)/shard_map/ppermute | solution.py:300
  32.5 4.6 %collective-permute-start.9 = (f32[168,128]{1,0:T(8,128)S(1)}, f32[168,128]{1,0:T(8,128)S(1)}, u32[]{:S(2)}, u32[]{:S(2)}) collective-permute-start(f32[168,128]{1,0:T(8,128)S(1)} %slice_add_fusion.own_ref), channel_id=1, source_target_pairs={{0,8},{8,0},{16,24},{24,16},{1,9},{9,1},{17,25},{25,17},{2,10},{10... | collective-permute-start | bytes 258056 | tf_op jit(solution)/shard_map/ppermute | solution.py:299
  35.7 1.3 %copy-start = (f32[128,20,128]{2,0,1:T(8,128)S(1)}, f32[128,20,128]{2,0,1:T(8,128)}, u32[]{:S(2)}) copy-start(f32[128,20,128]{2,0,1:T(8,128)} %param.9) | copy-start | bytes 3932164
  35.8 1.3 %copy-start.1 = (s32[128,128]{1,0:T(8,128)S(1)}, s32[128,128]{1,0:T(8,128)}, u32[]{:S(2)}) copy-start(s32[128,128]{1,0:T(8,128)} %cell_ref.3) | copy-start | bytes 196612
  35.8 1.3 %copy-start.2 = (f32[128,128]{1,0:T(8,128)S(1)}, f32[128,128]{1,0:T(8,128)}, u32[]{:S(2)}) copy-start(f32[128,128]{1,0:T(8,128)} %rate_ref.1) | copy-start | bytes 196612
